TPU v7x, 32 devices: a whole 2x2x4 slice. The times are simulated.
32 devices in a mesh: dp: 16 (over z, x, core), shard: 2 (over y).
Axes of the slice: x: 2, y: 2, z: 4, core: 2. Of those that a mesh axis runs over, the one named last changes fastest.
Arguments:
- tokens: bfloat16 [4096, 1088], P(('dp', 'shard')), may hold values from -6 to 6
- seq_ends: int32 [32, 3], P(('dp', 'shard')), may hold values from 0 to 128, as said below
- attn_weight: bfloat16 [1, 4352, 1088], P(None, ('dp', 'shard'))
- up_weight: bfloat16 [1, 4352, 1088], P(None, ('dp', 'shard')), may hold values from -0.1875 to 0.1875
- down_weight: bfloat16 [1, 4352, 1088], P(None, ('dp', 'shard')), may hold values from -0.09375 to 0.09375
- vectors: bfloat16 [1, 13056], P(None, ('dp', 'shard'))
- cotangent: bfloat16 [4096, 1088], P(('dp', 'shard')), may hold values from -6 to 6
Outputs:
- output: bfloat16 [4096, 1088], P(('dp', 'shard'))
- grad_tokens: float32 [4096, 1088], P(('dp', 'shard'))
- grad_attn: float32 [1, 4352, 1088], P(None, ('dp', 'shard'))
- grad_up: float32 [1, 4352, 1088], P(None, ('dp', 'shard'))
- grad_down: float32 [1, 4352, 1088], P(None, ('dp', 'shard'))
- grad_vectors: float32 [1, 13056], P(None, ('dp', 'shard'))
Inputs may be any that keep to these rules, and one draw needn't show every extreme that they name: `seq_ends`: each row lists non-decreasing end offsets of the sequences packed into one device's 128 slots; slots from the row's last end onward form one more segment.
All inputs are finite; a program needn't handle non-finite values.
Results may differ from a plain program's by a relative error of at most 0.0089.
Values may be sent and summed in bfloat16 or wider, within the bound.
A program may use at most 192 MiB of HBM per device.

v0:
```python
import jax
import jax.numpy as jnp
from jax import lax
from jax.sharding import PartitionSpec as P

HEAD_DIM = 64
EPS = 1e-05


def layer_norm(values, gain, shift):
    average = jnp.mean(values, axis=-1, keepdims=True)
    centred = values - average
    variance = jnp.mean(centred * centred, axis=-1, keepdims=True)
    return centred * lax.rsqrt(variance + EPS) * gain + shift


def gelu_tanh(values):
    return (
        0.5
        * values
        * (1.0 + jnp.tanh(0.7978845608028654 * (values + 0.044715 * values * values * values)))
    )


def contract_last(left, right):
    return lax.dot_general(
        left, right, (((1,), (1,)), ((), ())), preferred_element_type=jnp.float32
    )


def contract_first(left, right):
    return lax.dot_general(
        left, right, (((0,), (0,)), ((), ())), preferred_element_type=jnp.float32
    )


def head_product(form, left, right):
    return jnp.einsum(form, left, right, preferred_element_type=jnp.float32)


def causal_mask(ends_row, slot_count):
    positions = jnp.arange(slot_count, dtype=jnp.int32)
    segment = jnp.sum((ends_row[None, :] <= positions[:, None]).astype(jnp.int32), axis=1)
    return (segment[:, None] == segment[None, :]) & (positions[None, :] <= positions[:, None])


def split_vectors(vectors, model_width):
    vector_f32 = vectors.astype(jnp.float32)
    parts_list = [
        vector_f32[slot_idx * model_width : (slot_idx + 1) * model_width] for slot_idx in range(8)
    ]
    return parts_list + [vector_f32[8 * model_width :]]


def forward_layer(hidden, params, allowed):
    attn_part, up_part, down_part, vector_part = params
    model_width = attn_part.shape[1]
    head_count = model_width // HEAD_DIM
    row_count = hidden.shape[0]
    (
        gain_one,
        shift_one,
        query_bias,
        value_bias,
        out_bias,
        gain_two,
        shift_two,
        down_bias,
        up_bias,
    ) = split_vectors(vector_part, model_width)
    normed_one = layer_norm(hidden, gain_one, shift_one).astype(jnp.bfloat16)
    projected = contract_last(normed_one, attn_part[: 3 * model_width])
    query_heads = (
        ((projected[:, :model_width] + query_bias) * HEAD_DIM ** (-0.5))
        .astype(jnp.bfloat16)
        .reshape(row_count, head_count, HEAD_DIM)
    )
    key_heads = (
        projected[:, model_width : 2 * model_width]
        .astype(jnp.bfloat16)
        .reshape(row_count, head_count, HEAD_DIM)
    )
    value_heads = (
        (projected[:, 2 * model_width :] + value_bias)
        .astype(jnp.bfloat16)
        .reshape(row_count, head_count, HEAD_DIM)
    )
    scores = jnp.where(allowed[None], head_product("qhc,khc->hqk", query_heads, key_heads), -1e30)
    log_total = jnp.log(jnp.sum(jnp.exp(scores), axis=-1))
    weights = jnp.exp(scores - log_total[..., None]).astype(jnp.bfloat16)
    context = (
        head_product("hqk,khc->qhc", weights, value_heads)
        .reshape(row_count, model_width)
        .astype(jnp.bfloat16)
    )
    after_attn = (
        hidden
        + jnp.dot(context, attn_part[3 * model_width :], preferred_element_type=jnp.float32)
        + out_bias
    )
    normed_two = layer_norm(after_attn, gain_two, shift_two).astype(jnp.bfloat16)
    pre_act = contract_last(normed_two, up_part) + up_bias
    activated = gelu_tanh(pre_act).astype(jnp.bfloat16)
    result = (
        after_attn + jnp.dot(activated, down_part, preferred_element_type=jnp.float32) + down_bias
    )
    saved_acts = (
        hidden,
        normed_one,
        query_heads,
        key_heads,
        value_heads,
        log_total,
        context,
        after_attn,
        normed_two,
        pre_act,
        activated,
    )
    return (result, saved_acts)


def backward_layer(upstream, params, saved_acts, allowed):
    attn_part, up_part, down_part, vector_part = params
    (
        hidden,
        normed_one,
        query_heads,
        key_heads,
        value_heads,
        log_total,
        context,
        after_attn,
        normed_two,
        pre_act,
        activated,
    ) = saved_acts
    model_width = attn_part.shape[1]
    head_count = model_width // HEAD_DIM
    row_count = hidden.shape[0]
    (
        gain_one,
        shift_one,
        query_bias,
        value_bias,
        out_bias,
        gain_two,
        shift_two,
        down_bias,
        up_bias,
    ) = split_vectors(vector_part, model_width)
    upstream_bf = upstream.astype(jnp.bfloat16)
    grad_down_bias = jnp.sum(upstream, axis=0)
    grad_act = contract_last(upstream_bf, down_part)
    grad_pre = jax.vjp(gelu_tanh, pre_act)[1](grad_act)[0]
    grad_up_bias = jnp.sum(grad_pre, axis=0)
    grad_pre_bf = grad_pre.astype(jnp.bfloat16)
    grad_normed_two = jnp.dot(grad_pre_bf, up_part, preferred_element_type=jnp.float32)
    back_two = jax.vjp(layer_norm, after_attn, gain_two, shift_two)[1]
    grad_mid, grad_gain_two, grad_shift_two = back_two(grad_normed_two)
    grad_mid = upstream + grad_mid
    grad_out_bias = jnp.sum(grad_mid, axis=0)
    grad_mid_bf = grad_mid.astype(jnp.bfloat16)
    grad_context = (
        contract_last(grad_mid_bf, attn_part[3 * model_width :])
        .astype(jnp.bfloat16)
        .reshape(row_count, head_count, HEAD_DIM)
    )
    scores = jnp.where(allowed[None], head_product("qhc,khc->hqk", query_heads, key_heads), -1e30)
    probs_f32 = jnp.exp(scores - log_total[..., None])
    probs_bf = probs_f32.astype(jnp.bfloat16)
    grad_values = head_product("hqk,qhc->khc", probs_bf, grad_context).reshape(
        row_count, model_width
    )
    grad_probs = head_product("qhc,khc->hqk", grad_context, value_heads)
    row_dot = jnp.sum(probs_f32 * grad_probs, axis=-1, keepdims=True)
    grad_scores = (probs_f32 * (grad_probs - row_dot)).astype(jnp.bfloat16)
    grad_query = head_product("hqk,khc->qhc", grad_scores, key_heads).reshape(
        row_count, model_width
    ) * HEAD_DIM ** (-0.5)
    grad_keys = head_product("hqk,qhc->khc", grad_scores, query_heads).reshape(
        row_count, model_width
    )
    grad_query_bias = jnp.sum(grad_query, axis=0)
    grad_value_bias = jnp.sum(grad_values, axis=0)
    grad_proj = jnp.concatenate([grad_query, grad_keys, grad_values], axis=1).astype(jnp.bfloat16)
    grad_normed_one = jnp.dot(
        grad_proj, attn_part[: 3 * model_width], preferred_element_type=jnp.float32
    )
    back_one = jax.vjp(layer_norm, hidden, gain_one, shift_one)[1]
    grad_below, grad_gain_one, grad_shift_one = back_one(grad_normed_one)
    grad_below = grad_mid + grad_below
    left_all = jnp.concatenate([grad_proj, context], axis=1)
    grad_vector = jnp.concatenate(
        [
            grad_gain_one,
            grad_shift_one,
            grad_query_bias,
            grad_value_bias,
            grad_out_bias,
            grad_gain_two,
            grad_shift_two,
            grad_down_bias,
            grad_up_bias,
        ]
    )
    operands = (left_all, normed_one, grad_mid_bf, grad_pre_bf, normed_two, activated, upstream_bf)
    return (grad_below, operands, grad_vector)


def shards(tokens, seq_ends, attn_weight, up_weight, down_weight, vectors, cotangent):
    allowed = causal_mask(seq_ends[0], tokens.shape[0])
    model_width = tokens.shape[1]
    attn_rows = attn_weight.shape[1]
    layer_count = attn_weight.shape[0]
    hidden = tokens.astype(jnp.float32)
    kept_params = []
    layer_idx = 0
    gathered = (
        lax.all_gather(attn_weight[layer_idx], ("dp", "shard"), axis=0, tiled=True),
        lax.all_gather(up_weight[layer_idx], ("dp", "shard"), axis=0, tiled=True),
        lax.all_gather(down_weight[layer_idx], ("dp", "shard"), axis=0, tiled=True),
        lax.all_gather(vectors[layer_idx], ("dp", "shard"), axis=0, tiled=True),
    )
    kept_params.append(gathered)
    hidden, saved_acts = forward_layer(hidden, gathered, allowed)
    saved_list = [saved_acts]
    output = hidden.astype(jnp.bfloat16)
    upstream = cotangent.astype(jnp.float32)
    grad_sets = [None] * layer_count
    for layer_idx in reversed(range(layer_count)):
        gathered = (
            lax.all_gather(attn_weight[layer_idx], ("dp", "shard"), axis=0, tiled=True),
            lax.all_gather(up_weight[layer_idx], ("dp", "shard"), axis=0, tiled=True),
            lax.all_gather(down_weight[layer_idx], ("dp", "shard"), axis=0, tiled=True),
            lax.all_gather(vectors[layer_idx], ("dp", "shard"), axis=0, tiled=True),
        )
        upstream, operands, grad_vector = backward_layer(
            upstream, gathered, saved_list[layer_idx], allowed
        )
        left_all, normed_one, grad_mid_bf, grad_pre_bf, normed_two, activated, upstream_bf = (
            operands
        )
        row_index = jnp.arange(attn_rows * lax.axis_size(("dp", "shard")), dtype=jnp.int32)
        first_rows = jnp.where(
            (row_index < 3 * model_width)[None, :], left_all, jnp.zeros_like(left_all)
        )
        second_rows = jnp.where(
            (row_index >= 3 * model_width)[None, :], left_all, jnp.zeros_like(left_all)
        )
        grad_attn_w = lax.psum_scatter(
            contract_first(first_rows, normed_one) + contract_first(second_rows, grad_mid_bf),
            ("dp", "shard"),
            scatter_dimension=0,
            tiled=True,
        )
        grad_up_w = lax.psum_scatter(
            contract_first(grad_pre_bf, normed_two),
            ("dp", "shard"),
            scatter_dimension=0,
            tiled=True,
        )
        grad_down_w = lax.psum_scatter(
            contract_first(activated, upstream_bf), ("dp", "shard"), scatter_dimension=0, tiled=True
        )
        grad_vec_own = lax.psum_scatter(
            grad_vector, ("dp", "shard"), scatter_dimension=0, tiled=True
        )
        grad_sets[layer_idx] = (grad_attn_w, grad_up_w, grad_down_w, grad_vec_own)
    grad_attn = jnp.stack([grad_sets[0][0]])
    grad_up = jnp.stack([grad_sets[0][1]])
    grad_down = jnp.stack([grad_sets[0][2]])
    grad_vectors = jnp.stack([grad_sets[0][3]])
    return (output, upstream, grad_attn, grad_up, grad_down, grad_vectors)


def solution(mesh):
    return jax.shard_map(
        shards,
        mesh=mesh,
        in_specs=(
            P(("dp", "shard"), None),
            P(("dp", "shard"), None),
            P(None, ("dp", "shard"), None),
            P(None, ("dp", "shard"), None),
            P(None, ("dp", "shard"), None),
            P(None, ("dp", "shard")),
            P(("dp", "shard"), None),
        ),
        out_specs=(
            P(("dp", "shard"), None),
            P(("dp", "shard"), None),
            P(None, ("dp", "shard"), None),
            P(None, ("dp", "shard"), None),
            P(None, ("dp", "shard"), None),
            P(None, ("dp", "shard")),
        ),
        check_vma=False,
    )
```

profile of v0, /device:TPU:0, one launch (start us, length us, event | category | flops | bytes accessed | tf_op | source)
XLA Modules:
  0.0 987.9 jit_solution(13790586589980789792)
XLA Ops:
  10.4 43.7 %all-reduce = bf16[13056]{0:T(1024)(128)(2,1)S(1)} all-reduce(bf16[13056]{0:T(1024)(128)(2,1)S(1)} %dynamic-update-slice), channel_id=2, replica_groups=mesh['dp'=16,'shard'=2] {'dp','shard'}, use_global_device_ids=true, to_apply=%add | all-reduce | flops 13056 | bytes 52224
  57.4 40.9 %all-gather.8.cloned.1.call-done = bf16[1,4352,1088]{2,1,0:T(8,128)(2,1)} async-done(((bf16[1,136,1088]{2,1,0:T(8,128)(2,1)}), bf16[1,4352,1088]{2,1,0:T(8,128)(2,1)}) %all-gather.8.cloned.1.call-update) | async-done | bytes 9469968 | tf_op jit(solution)/shard_map/all_gather | solution.py:220
  98.4 5.4 fusion.10
  105.2 3.0 fusion.94
  108.3 75.5 %all-gather.10.cloned.1.call-done = bf16[1,4352,1088]{2,1,0:T(8,128)(2,1)} async-done(((bf16[1,136,1088]{2,1,0:T(8,128)(2,1)}), bf16[1,4352,1088]{2,1,0:T(8,128)(2,1)}) %all-gather.10.cloned.1.call-update) | async-done | bytes 9469968 | tf_op jit(solution)/shard_map/all_gather | solution.py:221
  183.9 7.2 fusion.11
  191.1 78.3 %all-gather.12.cloned.1.call-done = bf16[1,4352,1088]{2,1,0:T(8,128)(2,1)} async-done(((bf16[1,136,1088]{2,1,0:T(8,128)(2,1)}), bf16[1,4352,1088]{2,1,0:T(8,128)(2,1)}) %all-gather.12.cloned.1.call-update) | async-done | bytes 9469968 | tf_op jit(solution)/shard_map/all_gather | solution.py:222
  269.4 7.4 fusion.97
  276.8 4.7 multiply_reduce_fusion.1
  282.8 3.3 convolution_convert_fusion
  286.1 3.0 fusion.92
  289.1 1.4 fusion.98
  290.5 1.3 multiply_reduce_fusion
  293.7 14.5 %fusion.35 = f32[4352,1088]{1,0:T(8,128)} fusion(pred[4352]{0:T(1024)(128)(4,1)S(1)} %iota_compare_fusion.2, bf16[128,1088]{0,1:T(8,128)(2,1)S(1)} %bitcast.88, bf16[128,1088]{0,1:T(8,128)(2,1)S(1)} %bitcast.85, bf16[128,1088]{0,1:T(8,128)(2,1)S(1)} %bitcast.74, bf16[128,1088]{0,1:T(8,128)(2,1)S(1)} %bitcast.77, bf16[128,1088]{0,1:T(8,128)(2,1)S(1)} %copy-done.1, ...), kind=kOutput, calls=%fused_computation.41 | convolution fusion | flops 1218002944 | bytes 20346624 | tf_op jit(solution)/shard_map/dot_general | solution.py:32
  308.2 20.0 %convolution_add_fusion = f32[4352,1088]{1,0:T(8,128)} fusion(f32[4352,1088]{1,0:T(8,128)} %fusion.35, bf16[128,1088]{0,1:T(8,128)(2,1)S(1)} %copy-done.18, pred[4352]{0:T(1024)(128)(4,1)S(1)} %iota_compare_fusion.1, bf16[128,1088]{0,1:T(8,128)(2,1)S(1)} %bitcast.89, bf16[128,1088]{0,1:T(8,128)(2,1)S(1)} %bitcast.86, bf16[128,1088]{0,1:T(8,128)(2,1)S(1)} %bitcast.75, ...), kind=kOutput, calls=%fused_computation.1 | convolution fusion | flops 1221902336 | bytes 39276800 | tf_op jit(solution)/shard_map/dot_general | solution.py:32
  328.2 12.6 %fusion.61 = f32[4352,1088]{1,0:T(8,128)} fusion(bf16[128,4352]{1,0:T(8,128)(2,1)} %copy-done.4, f32[128,1088]{0,1:T(8,128)S(1)} %get-tuple-element.33, f32[1088]{0:T(1024)S(1)} %get-tuple-element.16, f32[1088]{0:T(1024)S(1)} %get-tuple-element.15, f32[128]{0:T(128)S(1)} %fusion.81, f32[128]{0:T(128)S(1)} %broadcast_multiply_fusion), kind=kOutput, calls=%fused_computation.82 | convolution fusion | flops 1212850176 | bytes 20620800 | tf_op jit(solution)/shard_map/dot_general | solution.py:32
  340.9 11.0 %fusion.89 = f32[4352,1088]{1,0:T(8,128)} fusion(bf16[128,1088]{0,1:T(8,128)(2,1)} %param.13, f32[128,4352]{1,0:T(8,128)S(1)} %fusion.11), kind=kOutput, calls=%fused_computation.124 | convolution fusion | flops 1217167360 | bytes 21446656 | tf_op jit(solution)/shard_map/dot_general | solution.py:32
  352.1 7.2 fusion.90
  359.8 1.2 convert_reduce_fusion.1
  361.1 40.9 %all-reduce.4 = f32[13056]{0:T(1024)S(1)} all-reduce(f32[13056]{0:T(1024)S(1)} %concatenate.13), channel_id=9, replica_groups=mesh['dp'=16,'shard'=2] {'dp','shard'}, use_global_device_ids=true, to_apply=%region_23.24.clone | all-reduce | flops 13056 | bytes 104448
  402.6 8.3 fusion.21
  411.0 130.0 %reduce-scatter.10.cloned.1.call-done = f32[136,1088]{1,0:T(8,128)} async-done(((f32[4352,1088]{1,0:T(8,128)}), f32[136,1088]{1,0:T(8,128)}) %reduce-scatter.10.cloned.1.call-update) | async-done | bytes 591888
  540.9 219.9 %reduce-scatter.12.cloned.1.call-done = f32[136,1088]{1,0:T(8,128)} async-done(((f32[4352,1088]{1,0:T(8,128)}), f32[136,1088]{1,0:T(8,128)}) %reduce-scatter.12.cloned.1.call-update) | async-done | bytes 591888
  760.9 219.9 %reduce-scatter.14.cloned.1.call-done = f32[136,1088]{1,0:T(8,128)} async-done(((f32[4352,1088]{1,0:T(8,128)}), f32[136,1088]{1,0:T(8,128)}) %reduce-scatter.14.cloned.1.call-update) | async-done | bytes 591888
  (89 shorter events, 12.3 us)
Async XLA Ops:
  7.2 91.2 %all-gather.8.cloned.1.call-start = ((), (), s32[]{:S(2)}) async-start(), calls=%async_computation.3 | async-start | bytes 10340352 | tf_op jit(solution)/shard_map/all_gather | solution.py:220
  7.9 176.0 %all-gather.10.cloned.1.call-start = ((), (), s32[]{:S(2)}) async-start(), calls=%async_computation.4 | async-start | bytes 10340352 | tf_op jit(solution)/shard_map/all_gather | solution.py:221
  8.6 260.7 %all-gather.12.cloned.1.call-start = ((), (), s32[]{:S(2)}) async-start(), calls=%async_computation.5 | async-start | bytes 10340352 | tf_op jit(solution)/shard_map/all_gather | solution.py:222
  9.4 531.5 %reduce-scatter.10.cloned.1.call-start = ((), (), s32[]{:S(2)}) async-start(), calls=%async_computation.6 | async-start | bytes 20680704
  103.9 1.3 copy-start.10
  103.9 1.3 copy-start.1
  104.3 3.9 copy-start.19
  104.6 3.5 copy-start.5
  105.1 3.2 copy-start.15
  183.9 85.5 %copy-start.12 = (bf16[128,1088]{0,1:T(8,128)(2,1)S(1)}, bf16[128,1088]{0,1:T(8,128)(2,1)}, u32[]{:S(2)}) copy-start(bf16[128,1088]{0,1:T(8,128)(2,1)} %param.13) | copy-start | bytes 835588
  269.4 7.5 copy-start
  276.8 4.8 copy-start.4
  282.7 3.4 copy-start.17
  282.7 6.4 copy-start.20
  289.1 1.4 copy-start.6
  291.9 1.4 copy-start.11
  291.9 1.8 copy-start.14
  291.9 1.8 copy-start.16
  293.7 14.5 %copy-start.7 = (bf16[17,64,128]{2,1,0:T(8,128)(2,1)}, bf16[17,64,128]{2,1,0:T(8,128)(2,1)S(1)}, u32[]{:S(2)}) copy-start(bf16[17,64,128]{2,1,0:T(8,128)(2,1)S(1)} %get-tuple-element.31) | copy-start | bytes 835588
  293.7 14.5 %copy-start.18 = (bf16[128,1088]{0,1:T(8,128)(2,1)S(1)}, bf16[128,1088]{0,1:T(8,128)(2,1)}, u32[]{:S(2)}) copy-start(bf16[128,1088]{0,1:T(8,128)(2,1)} %copy-done.17) | copy-start | bytes 835588
  328.2 432.7 %reduce-scatter.12.cloned.1.call-start = ((), (), s32[]{:S(2)}) async-start(), calls=%async_computation.7 | async-start | bytes 20680704
  340.8 639.9 %reduce-scatter.14.cloned.1.call-start = ((), (), s32[]{:S(2)}) async-start(), calls=%async_computation.8 | async-start | bytes 20680704
  352.1 7.7 copy-start.3
  352.1 7.7 copy-start.13
  (3 other events, 2.7 us)
Sparse Core Ops, SparseCore 0:
  10.8 87.5 all-gather.7
  101.2 82.5 all-gather.9
  186.7 82.5 all-gather.11
  328.3 212.5 reduce-scatter.9
  547.8 213.0 reduce-scatter.11
  767.7 213.0 reduce-scatter.13
where the time goes:
time: 998 us; the launch traced here: 988 us
  waiting for transfers between devices  767 us (77%)
  matrix products  111 us (11%)
  blocking collectives  84.6 us (8%)
  between operations  14.8 us (1%)
    unnamed x9, waiting for transfers between devices  572 us
    unnamed x2, blocking collectives  84.6 us
    all_gather x1, waiting for transfers between devices, shards(): lax.all_gather(down_weight[layer_idx], ('dp', 'shard'), axis=0, tiled=True)  78.3 us
    all_gather x1, waiting for transfers between devices, shards(): lax.all_gather(up_weight[layer_idx], ('dp', 'shard'), axis=0, tiled=True)  75.5 us
    dot_general x4, matrix products, contract_first(): lax.dot_general(left, right, (((0,), (0,)), ((), ())), preferred_element_...  58 us
    all_gather x1, waiting for transfers between devices, shards(): lax.all_gather(attn_weight[layer_idx], ('dp', 'shard'), axis=0, tiled=True)  40.9 us
    dot_general x4, matrix products, contract_last(): lax.dot_general(left, right, (((1,), (1,)), ((), ())), preferred_element_...  23.5 us
  transfers between devices with their start and end apart: 6, of which 6 were waited for; matrix products, arithmetic and copies ran while one was open for 6% of the time, Pallas kernels for 0%

commit v1 on v0

--- a/solution.py
+++ b/solution.py
@@ -5,6 +5,12 @@
 
 HEAD_DIM = 64
 EPS = 1e-05
+
+
+def gather_by_exchange(x, axis, dim):
+    count = lax.axis_size(axis)
+    repeats = [count if d == dim else 1 for d in range(x.ndim)]
+    return lax.all_to_all(jnp.tile(x, repeats), axis, split_axis=dim, concat_axis=dim, tiled=True)
 
 
 def layer_norm(values, gain, shift):
@@ -219,7 +225,7 @@
     gathered = (
         lax.all_gather(attn_weight[layer_idx], ("dp", "shard"), axis=0, tiled=True),
         lax.all_gather(up_weight[layer_idx], ("dp", "shard"), axis=0, tiled=True),
-        lax.all_gather(down_weight[layer_idx], ("dp", "shard"), axis=0, tiled=True),
+        gather_by_exchange(down_weight[layer_idx], ("dp", "shard"), 0),
         lax.all_gather(vectors[layer_idx], ("dp", "shard"), axis=0, tiled=True),
     )
     kept_params.append(gathered)

time: 998 us -> 1120 us (1.12)
  blocking collectives: 84.6 us -> 371 us
  waiting for transfers between devices: 767 us -> 599 us
    unnamed x2, blocking collectives: 84.6 us -> 371 us
    unnamed x9, waiting for transfers between devices: 572 us -> 404 us
  transfers between devices with their start and end apart: 6 -> 7, of which waited for: 6 -> 5; matrix products, arithmetic and copies ran while one was open for 6% -> 6% of each run, Pallas kernels for 0% -> 0%
where the time goes in v1:
time: 1120 us; the launch traced here: 1110 us
  waiting for transfers between devices  599 us (53%)
  blocking collectives  371 us (33%)
  matrix products  107 us (10%)
  between operations  14.7 us (1%)
  local copies, waits for them, and re-layouts  11.4 us (1%)
    unnamed x9, waiting for transfers between devices  404 us
    unnamed x2, blocking collectives  371 us
    all_gather x1, waiting for transfers between devices, shards(): lax.all_gather(down_weight[layer_idx], ('dp', 'shard'), axis=0, tiled=True)  78.3 us
    all_gather x1, waiting for transfers between devices, shards(): lax.all_gather(up_weight[layer_idx], ('dp', 'shard'), axis=0, tiled=True)  74.8 us
    dot_general x4, matrix products, contract_first(): lax.dot_general(left, right, (((0,), (0,)), ((), ())), preferred_element_...  54.3 us
    all_gather x1, waiting for transfers between devices, shards(): lax.all_gather(attn_weight[layer_idx], ('dp', 'shard'), axis=0, tiled=True)  40.9 us
    dot_general x4, matrix products, contract_last(): lax.dot_general(left, right, (((1,), (1,)), ((), ())), preferred_element_...  22.7 us
  transfers between devices with their start and end apart: 7, of which 5 were waited for; matrix products, arithmetic and copies ran while one was open for 6% of the time, Pallas kernels for 0%

profile of v1, /device:TPU:0, one launch (start us, length us, event | category | flops | bytes accessed | tf_op | source)
XLA Modules:
  0.0 1113.8 jit_solution(16578234807698125536)
XLA Ops:
  10.4 43.7 %all-reduce = bf16[13056]{0:T(1024)(128)(2,1)S(1)} all-reduce(bf16[13056]{0:T(1024)(128)(2,1)S(1)} %dynamic-update-slice), channel_id=2, replica_groups=mesh['dp'=16,'shard'=2] {'dp','shard'}, use_global_device_ids=true, to_apply=%add | all-reduce | flops 13056 | bytes 52224
  57.4 40.9 %all-gather.8.cloned.1.call-done = bf16[1,4352,1088]{2,1,0:T(8,128)(2,1)} async-done(((bf16[1,136,1088]{2,1,0:T(8,128)(2,1)}), bf16[1,4352,1088]{2,1,0:T(8,128)(2,1)}) %all-gather.8.cloned.1.call-update) | async-done | bytes 9469968 | tf_op jit(solution)/shard_map/all_gather | solution.py:226
  98.4 5.4 fusion.8
  105.8 3.0 fusion.85
  109.0 74.8 %all-gather.10.cloned.1.call-done = bf16[1,4352,1088]{2,1,0:T(8,128)(2,1)} async-done(((bf16[1,136,1088]{2,1,0:T(8,128)(2,1)}), bf16[1,4352,1088]{2,1,0:T(8,128)(2,1)}) %all-gather.10.cloned.1.call-update) | async-done | bytes 9469968 | tf_op jit(solution)/shard_map/all_gather | solution.py:227
  183.8 7.2 fusion.9
  191.1 78.3 %all-gather.12.cloned.1.call-done = bf16[1,4352,1088]{2,1,0:T(8,128)(2,1)} async-done(((bf16[1,136,1088]{2,1,0:T(8,128)(2,1)}), bf16[1,4352,1088]{2,1,0:T(8,128)(2,1)}) %all-gather.12.cloned.1.call-update) | async-done | bytes 9469968 | tf_op jit(solution)/shard_map/all_gather | solution.py:241
  269.3 7.4 fusion.88
  276.8 4.7 multiply_reduce_fusion.1
  283.4 2.6 convolution_convert_fusion
  287.4 1.2 multiply_reduce_fusion
  291.2 2.9 fusion.83
  294.1 11.0 fusion.26
  305.1 20.0 %convolution_add_fusion = f32[4352,1088]{1,0:T(8,128)} fusion(f32[4352,1088]{1,0:T(8,128)} %fusion.26, bf16[128,1088]{0,1:T(8,128)(2,1)S(1)} %copy-done.18, pred[4352]{0:T(1024)(128)(4,1)S(1)} %iota_compare_fusion.1, bf16[128,1088]{0,1:T(8,128)(2,1)S(1)} %bitcast.85, bf16[128,1088]{0,1:T(8,128)(2,1)S(1)} %bitcast.82, bf16[128,1088]{0,1:T(8,128)(2,1)S(1)} %bitcast.74, ...), kind=kOutput, calls=%fused_computation.1 | convolution fusion | flops 1221902336 | bytes 39276800 | tf_op jit(solution)/shard_map/dot_general | solution.py:38
  325.2 12.6 %fusion.52 = f32[4352,1088]{1,0:T(8,128)} fusion(bf16[128,4352]{1,0:T(8,128)(2,1)} %copy-done.4, f32[128,1088]{0,1:T(8,128)S(1)} %get-tuple-element.33, f32[1088]{0:T(1024)S(1)} %get-tuple-element.16, f32[1088]{0:T(1024)S(1)} %get-tuple-element.15, f32[128]{0:T(128)S(1)} %fusion.72, f32[128]{0:T(128)S(1)} %broadcast_multiply_fusion), kind=kOutput, calls=%fused_computation.80 | convolution fusion | flops 1212850176 | bytes 20620800 | tf_op jit(solution)/shard_map/dot_general | solution.py:38
  337.8 10.8 fusion.80
  348.6 6.1 tile.9
  354.7 4.0 all-to-all-start
  358.8 7.2 fusion.81
  366.5 1.2 convert_reduce_fusion.1
  367.8 326.9 %all-reduce.4 = f32[13056]{0:T(1024)S(1)} all-reduce(f32[13056]{0:T(1024)S(1)} %concatenate.13), channel_id=9, replica_groups=mesh['dp'=16,'shard'=2] {'dp','shard'}, use_global_device_ids=true, to_apply=%region_23.24.clone | all-reduce | flops 13056 | bytes 104448
  695.4 8.9 fusion.14
  704.3 182.4 %reduce-scatter.12.cloned.1.call-done = f32[136,1088]{1,0:T(8,128)} async-done(((f32[4352,1088]{1,0:T(8,128)}), f32[136,1088]{1,0:T(8,128)}) %reduce-scatter.12.cloned.1.call-update) | async-done | bytes 591888
  886.8 219.9 %reduce-scatter.14.cloned.1.call-done = f32[136,1088]{1,0:T(8,128)} async-done(((f32[4352,1088]{1,0:T(8,128)}), f32[136,1088]{1,0:T(8,128)}) %reduce-scatter.14.cloned.1.call-update) | async-done | bytes 591888
  (94 shorter events, 15.7 us)
Async XLA Ops:
  7.2 91.2 %all-gather.8.cloned.1.call-start = ((), (), s32[]{:S(2)}) async-start(), calls=%async_computation.4 | async-start | bytes 10340352 | tf_op jit(solution)/shard_map/all_gather | solution.py:226
  7.9 175.9 %all-gather.10.cloned.1.call-start = ((), (), s32[]{:S(2)}) async-start(), calls=%async_computation.5 | async-start | bytes 10340352 | tf_op jit(solution)/shard_map/all_gather | solution.py:227
  8.6 260.7 %all-gather.12.cloned.1.call-start = ((), (), s32[]{:S(2)}) async-start(), calls=%async_computation.6 | async-start | bytes 10340352 | tf_op jit(solution)/shard_map/all_gather | solution.py:241
  9.4 694.9 %reduce-scatter.10.cloned.1.call-start = ((), (), s32[]{:S(2)}) async-start(), calls=%async_computation.7 | async-start | bytes 20680704
  103.9 1.5 copy-start.10
  103.9 2.0 copy-start.1
  104.3 1.6 copy-start.19
  105.3 3.5 copy-start.5
  105.8 3.2 copy-start.15
  183.8 85.5 %copy-start.12 = (bf16[128,1088]{0,1:T(8,128)(2,1)S(1)}, bf16[128,1088]{0,1:T(8,128)(2,1)}, u32[]{:S(2)}) copy-start(bf16[128,1088]{0,1:T(8,128)(2,1)} %param.13) | copy-start | bytes 835588
  269.3 7.5 copy-start
  276.8 4.8 copy-start.4
  283.4 2.6 copy-start.20
  286.0 2.6 copy-start.21
  286.0 1.4 copy-start.6
  294.1 11.0 copy-start.7
  294.1 11.0 copy-start.14
  294.1 11.0 copy-start.16
  294.1 11.0 copy-start.18
  325.1 561.6 %reduce-scatter.12.cloned.1.call-start = ((), (), s32[]{:S(2)}) async-start(), calls=%async_computation.8 | async-start | bytes 20680704
  337.8 768.9 %reduce-scatter.14.cloned.1.call-start = ((), (), s32[]{:S(2)}) async-start(), calls=%async_computation.9 | async-start | bytes 20680704
  354.7 340.7 %all-to-all-start = ((bf16[32,136,1088]{2,1,0:T(8,128)(2,1)}), bf16[32,136,1088]{2,1,0:T(8,128)(2,1)}, u32[]{:S(2)}, u32[]{:S(2)}) async-start(bf16[32,136,1088]{2,1,0:T(8,128)(2,1)} %tile.9), calls=%async_computation | async-start | bytes 20054016 | tf_op jit(solution)/shard_map/all_to_all | solution.py:13
  358.8 7.7 copy-start.3
  358.8 7.7 copy-start.13
  (5 other events, 4.5 us)
Sparse Core Ops, SparseCore 0:
  10.8 87.5 all-gather.7
  101.2 82.5 all-gather.9
  186.7 82.5 all-gather.11
  325.2 341.7 reduce-scatter.9
  673.9 212.7 reduce-scatter.11
  893.6 213.0 reduce-scatter.13
